TPU v7x, 512 devices: a whole 4x8x8 slice. The times are simulated.
512 devices in a mesh: sta: 128 (over z_hi, y, x, core), cell: 4 (over z_lo).
Axes of the slice: x: 4, y: 8, z: 8 (z_hi: 2, z_lo: 4; z = z_hi * 4 + z_lo), core: 2. Of those that a mesh axis runs over, the one named last changes fastest.
Arguments:
- sensitivity: bfloat16 [2048, 52, 2048], P('sta', None, 'cell'), may hold values from -0.01953125 to 0.01953125
- footprint: int32 [128, 52], P('sta'), may hold values from 0 to 63, as said below
- linked: int32 [128, 9], P('sta'), may hold values from 0 to 1, as said below
- smooth_x: bfloat16 [16, 16], replicated, may hold values from 0 to 8, as said below
- smooth_y: bfloat16 [64, 64], replicated, may hold values from 0 to 8, as said below
- smooth_z: bfloat16 [128, 128], replicated, may hold values from 0 to 8, as said below
Outputs:
- band: float32 [2048, 144], P('sta', 'cell')
Inputs may be any that keep to these rules, and one draw needn't show every extreme that they name: `footprint`: within a row the 52 tiles are different. linked[b, 4] is 1, and linked[b, 4 + k] equals linked[(b + k) mod the number of row blocks, 4 - k] for 1 <= k <= 4. `smooth_x`: Symmetric, with positive entries. `smooth_y`: Symmetric, with positive entries. `smooth_z`: Symmetric, with positive entries.
All inputs are finite; a program needn't handle non-finite values.
Results may differ from a plain program's by a relative error of at most 0.005.
Values may be sent and summed in bfloat16 or wider, within the bound.
A program may use at most 64 MiB of HBM per device.

v0:
```python
import math
import jax
import jax.numpy as jnp
from jax import lax
from jax.sharding import PartitionSpec as P

TILE = 16
HALF = 4
TILES = 64
BAND = 9


def from_behind(block, axis, distance):
    devices = range(lax.axis_size(axis))
    route = [((i - distance) % len(devices), i) for i in devices]
    return lax.ppermute(block, axis, route)


def in_blocks(array, dim, size):
    before, after = (array.shape[:dim], array.shape[dim + 1 :])
    return jnp.moveaxis(array.reshape(*before, size, -1, *after), dim, 0)


def sent_and_summed(array, axis, dim):
    blocks = in_blocks(array, dim, lax.axis_size(axis))
    arrived = lax.all_to_all(blocks, axis, split_axis=0, concat_axis=0, tiled=True)
    return arrived.sum(axis=0)


def spread_tiles(values, foot_tiles):
    onehot = (foot_tiles[:, None] == jnp.arange(TILES, dtype=jnp.int32)[None, :]).astype(
        jnp.bfloat16
    )
    placed = jnp.einsum("rfk,ft->rtk", values, onehot, preferred_element_type=jnp.float32)
    return placed.astype(jnp.bfloat16)


def smooth_depth(block, smooth_z):
    row_count, tile_count, slab_width = block.shape
    depth_cells = smooth_z.shape[0]
    grid_field = block.reshape(row_count, tile_count, depth_cells, slab_width // depth_cells)
    smoothed = jnp.einsum("rtzc,wz->rtwc", grid_field, smooth_z, preferred_element_type=jnp.float32)
    return smoothed.astype(jnp.bfloat16).reshape(row_count, tile_count, slab_width)


def smooth_plane(field_rows, smooth_x, smooth_y):
    row_count, tile_count, slab_width = field_rows.shape
    cells_across = smooth_x.shape[0]
    blocks_along = tile_count // cells_across
    group_rows = math.gcd(row_count, 4)
    y_kernel = smooth_y.reshape(blocks_along, TILE, blocks_along, TILE)

    def smooth_group(row_group):
        grid_field = row_group.reshape(
            group_rows, cells_across, blocks_along, slab_width // TILE, TILE
        )
        across = jnp.einsum(
            "rxbzc,vx->rvbzc", grid_field, smooth_x, preferred_element_type=jnp.float32
        ).astype(jnp.bfloat16)
        along = jnp.einsum(
            "rxbzc,ekbc->rxezk", across, y_kernel, preferred_element_type=jnp.float32
        ).astype(jnp.bfloat16)
        return along.reshape(group_rows, tile_count, slab_width)

    grouped = field_rows.reshape(row_count // group_rows, group_rows, tile_count, slab_width)
    return lax.map(smooth_group, grouped).reshape(row_count, tile_count, slab_width)


def pair_tile(smoothed, values, foot_tiles):
    row_count = smoothed.shape[0]
    picked = jnp.take(smoothed, foot_tiles, axis=1).reshape(row_count, -1)
    partner = values.reshape(values.shape[0], -1)
    return lax.dot_general(
        picked, partner, (((1,), (1,)), ((), ())), preferred_element_type=jnp.float32
    )


def body(sensitivity, footprint, linked, smooth_x, smooth_y, smooth_z):
    own_tiles = footprint[0]
    depth_rows = lax.all_to_all(
        smooth_depth(
            lax.all_to_all(sensitivity, "cell", split_axis=1, concat_axis=2, tiled=True), smooth_z
        ),
        "cell",
        split_axis=2,
        concat_axis=1,
        tiled=True,
    )
    grid_rows = spread_tiles(depth_rows, own_tiles)
    smoothed = smooth_plane(grid_rows, smooth_x, smooth_y)
    pair_flags = linked[0]

    def masked_tile(values, foot_tiles, flag):
        return pair_tile(smoothed, values, foot_tiles) * flag.astype(jnp.float32)

    band_parts = [None] * BAND
    band_parts[HALF] = masked_tile(sensitivity, own_tiles, pair_flags[HALF])
    carried = (sensitivity, footprint)
    for offset in range(1, HALF + 1):
        carried = from_behind((carried[0], carried[1]), "sta", 1)
        band_parts[HALF - offset] = masked_tile(
            carried[0], carried[1][0], pair_flags[HALF - offset]
        )
    for offset in range(1, HALF + 1):
        band_parts[HALF + offset] = from_behind(band_parts[HALF - offset].T, "sta", -offset)
    partial_band = jnp.concatenate(band_parts, axis=1)
    return sent_and_summed(partial_band, "cell", 1)


def solution(mesh):
    return jax.shard_map(
        body,
        mesh=mesh,
        in_specs=(P("sta", None, "cell"), P("sta", None), P("sta", None), P(), P(), P()),
        out_specs=P("sta", "cell"),
        check_vma=False,
    )
```

profile of v0, /device:TPU:62, one launch (start us, length us, event | category | flops | bytes accessed | tf_op | source)
XLA Modules:
  0.0 227.8 jit_solution(7614213136167638222)
XLA Ops:
  0.0 7.4 %all-to-all-start = ((bf16[16,52,512]{2,0,1:T(8,128)(2,1)}), bf16[16,52,512]{2,0,1:T(8,128)(2,1)S(1)}, u32[]{:S(2)}, u32[]{:S(2)}) async-start(bf16[16,52,512]{2,0,1:T(8,128)(2,1)} %param.10), calls=%async_computation | async-start | bytes 1703936 | tf_op jit(solution)/shard_map/all_to_all | solution.py:82
  7.4 1.9 collective-permute-start.4
  9.3 7.4 %collective-permute-start = (s32[1,52]{1,0:T(1,128)}, s32[1,52]{1,0:T(1,128)S(1)}, u32[]{:S(2)}, u32[]{:S(2)}) collective-permute-start(s32[1,52]{1,0:T(1,128)} %param.11), channel_id=1, source_target_pairs={{508,0},{0,4},{4,8},{8,12},{12,16},{16,20},{20,24},{24,28},{28,32}... | collective-permute-start | bytes 632 | tf_op jit(solution)/shard_map/ppermute | solution.py:16
  16.8 0.8 reshape.59
  17.6 1.5 fusion.41
  20.9 0.7 compare_select_fusion
  21.6 0.7 compare_and_fusion
  23.5 9.2 %collective-permute-start.1 = (s32[1,52]{1,0:T(1,128)S(1)}, s32[1,52]{1,0:T(1,128)S(1)}, u32[]{:S(2)}, u32[]{:S(2)}) collective-permute-start(s32[1,52]{1,0:T(1,128)S(1)} %collective-permute-done), channel_id=1, source_target_pairs={{508,0},{0,4},{4,8},{8,12},{12,16},{16,20},{20,24},{24,28},{28,32}... | collective-permute-start | bytes 632 | tf_op jit(solution)/shard_map/ppermute | solution.py:16
  32.7 0.8 collective-permute-done.1
  33.5 15.7 %collective-permute-start.2 = (s32[1,52]{1,0:T(1,128)S(1)}, s32[1,52]{1,0:T(1,128)S(1)}, u32[]{:S(2)}, u32[]{:S(2)}) collective-permute-start(s32[1,52]{1,0:T(1,128)S(1)} %collective-permute-done.1), channel_id=1, source_target_pairs={{508,0},{0,4},{4,8},{8,12},{12,16},{16,20},{20,24},{24,28},{28,32}... | collective-permute-start | bytes 632 | tf_op jit(solution)/shard_map/ppermute | solution.py:16
  49.2 12.3 %collective-permute-start.5 = (bf16[16,52,512]{2,0,1:T(8,128)(2,1)S(1)}, bf16[16,52,512]{2,0,1:T(8,128)(2,1)}, u32[]{:S(2)}, u32[]{:S(2)}) collective-permute-start(bf16[16,52,512]{2,0,1:T(8,128)(2,1)S(1)} %collective-permute-done.4), channel_id=1, source_target_pairs={{508,0},{0,4},{4,8},{8,12},{12,16},{16,20},{20,24},{24,28},{28,32}... | collective-permute-start | bytes 2555912 | tf_op jit(solution)/shard_map/ppermute | solution.py:16
  61.5 0.7 copy.73
  62.2 6.1 %reshape.56 = bf16[16,13,128,16]{3,2,1,0:T(8,128)(2,1)} reshape(bf16[16,13,4,512]{3,2,1,0:T(4,128)(2,1)S(1)} %bitcast.140) | data formatting | bytes 1703936 | tf_op jit(solution)/shard_map/reshape | solution.py:41
  68.3 4.8 %fusion.5 = bf16[16,13,128,16]{2,3,1,0:T(8,128)(2,1)S(1)} fusion(bf16[16,13,128,16]{3,2,1,0:T(8,128)(2,1)} %reshape.56, bf16[128,128]{1,0:T(8,128)(2,1)S(1)} %copy-done), kind=kOutput, calls=%fused_computation.16 | convolution fusion | flops 109477888 | bytes 1736704 | tf_op jit(solution)/shard_map/rtzc,wz->rtwc/dot_general | solution.py:42
  73.2 12.5 %copy.60 = bf16[16,13,128,16]{0,1,3,2:T(8,128)(2,1)} copy(bf16[16,13,128,16]{2,3,1,0:T(8,128)(2,1)S(1)} %fusion.5) | data formatting | bytes 1703936 | tf_op jit(solution)/shard_map/reshape | solution.py:43
  85.7 8.3 %reshape.128 = bf16[4,2,53248]{2,1,0:T(2,128)(2,1)} reshape(bf16[2048,13,16]{2,1,0:T(8,128)(2,1)} %bitcast.135) | data formatting | bytes 1703936
  94.0 5.8 %all-to-all-start.1 = ((bf16[4,2,53248]{2,1,0:T(2,128)(2,1)}), bf16[4,2,53248]{2,1,0:T(2,128)(2,1)S(1)}, u32[]{:S(2)}, u32[]{:S(2)}) async-start(bf16[4,2,53248]{2,1,0:T(2,128)(2,1)} %reshape.128), calls=%async_computation.1 | async-start | bytes 1703936 | tf_op jit(solution)/shard_map/all_to_all | solution.py:80
  99.9 1.9 collective-permute-start.3
  101.8 2.1 collective-permute-start.6
  104.0 0.8 collective-permute-done.3
  104.8 16.7 %all-to-all-done.1 = bf16[4,2,53248]{2,1,0:T(2,128)(2,1)S(1)} async-done(((bf16[4,2,53248]{2,1,0:T(2,128)(2,1)}), bf16[4,2,53248]{2,1,0:T(2,128)(2,1)S(1)}, u32[]{:S(2)}, u32[]{:S(2)}) %all-to-all-start.1) | async-done | bytes 852000 | tf_op jit(solution)/shard_map/all_to_all | solution.py:80
  121.5 7.7 %reshape.129 = bf16[2048,13,16]{2,1,0:T(8,128)(2,1)} reshape(bf16[4,2,53248]{2,1,0:T(2,128)(2,1)S(1)} %all-to-all-done.1) | data formatting | bytes 1703936
  129.3 9.3 %copy.61 = bf16[16,13,4,512]{3,2,0,1:T(4,128)(2,1)S(1)} copy(bf16[16,13,4,512]{0,1,3,2:T(8,128)(2,1)} %bitcast.136) | data formatting | bytes 1703936 | tf_op jit(solution)/shard_map/all_to_all | solution.py:80
  138.8 2.3 convolution_convert_fusion.1
  141.0 1.9 collective-permute-start.7
  143.0 40.5 %while.10 = (s32[]{:T(128)}, bf16[4,4,64,512]{3,2,1,0:T(8,128)(2,1)}, bf16[4,4,64,512]{3,2,1,0:T(8,128)(2,1)}, bf16[16,16]{1,0:T(8,128)(2,1)S(1)}, bf16[4,16,4,16]{3,1,2,0:T(8,128)(2,1)S(1)}, /*index=5*/s32[]{:T(128)}) while((s32[]{:T(128)}, bf16[4,4,64,512]{3,2,1,0:T(8,128)(2,1)}, bf16[4,4,64,512]{3,2,1,0:T(8,128)(2,1)}, ...), condition=%wide.region_1.2_spmd, body=%wide.region_0.1_spmd.sunk | while | flops 21233664 | bytes 4203593 | solution.py:66
  143.0 1.0 constant_dynamic-slice_fusion.2
  144.0 1.7 reshape.133
  145.7 1.2 copy.79
  147.7 1.0 copy.80
  148.8 3.6 %broadcast_in_dim.31 = bf16[1,4,64,512]{3,2,1,0:T(8,128)(2,1)S(1)} reshape(bf16[4,16,4,32,16]{4,3,2,1,0:T(8,128)(2,1)S(1)} %copy.80) | data formatting | bytes 524288 | tf_op jit(solution)/shard_map/while/body/jit(dynamic_update_index_in_dim)/broadcast_in_dim | solution.py:66
  152.4 0.7 constant_dynamic-update-slice_fusion.2
  153.1 1.0 constant_dynamic-slice_fusion.2
  154.1 1.7 reshape.133
  155.8 1.2 copy.79
  157.9 1.0 copy.80
  158.9 3.6 %broadcast_in_dim.31 = bf16[1,4,64,512]{3,2,1,0:T(8,128)(2,1)S(1)} reshape(bf16[4,16,4,32,16]{4,3,2,1,0:T(8,128)(2,1)S(1)} %copy.80) | data formatting | bytes 524288 | tf_op jit(solution)/shard_map/while/body/jit(dynamic_update_index_in_dim)/broadcast_in_dim | solution.py:66
  162.5 0.7 constant_dynamic-update-slice_fusion.2
  163.2 1.0 constant_dynamic-slice_fusion.2
  164.2 1.7 reshape.133
  165.9 1.2 copy.79
  168.0 1.0 copy.80
  169.0 3.6 %broadcast_in_dim.31 = bf16[1,4,64,512]{3,2,1,0:T(8,128)(2,1)S(1)} reshape(bf16[4,16,4,32,16]{4,3,2,1,0:T(8,128)(2,1)S(1)} %copy.80) | data formatting | bytes 524288 | tf_op jit(solution)/shard_map/while/body/jit(dynamic_update_index_in_dim)/broadcast_in_dim | solution.py:66
  172.6 0.7 constant_dynamic-update-slice_fusion.2
  173.4 1.0 constant_dynamic-slice_fusion.2
  174.3 1.7 reshape.133
  176.0 1.2 copy.79
  178.1 1.0 copy.80
  179.2 3.6 %broadcast_in_dim.31 = bf16[1,4,64,512]{3,2,1,0:T(8,128)(2,1)S(1)} reshape(bf16[4,16,4,32,16]{4,3,2,1,0:T(8,128)(2,1)S(1)} %copy.80) | data formatting | bytes 524288 | tf_op jit(solution)/shard_map/while/body/jit(dynamic_update_index_in_dim)/broadcast_in_dim | solution.py:66
  182.8 0.7 constant_dynamic-update-slice_fusion.2
  183.5 1.8 copy.62
  185.3 0.6 gather_fusion
  186.6 1.7 fusion.9
  188.3 1.9 collective-permute-start.10
  190.8 1.7 fusion.8
  192.6 1.9 collective-permute-start.9
  195.1 1.7 fusion.7
  196.8 3.7 %collective-permute-start.8 = (f32[16,16]{1,0:T(8,128)S(1)}, f32[16,16]{1,0:T(8,128)S(1)}, u32[]{:S(2)}, u32[]{:S(2)}) collective-permute-start(f32[16,16]{1,0:T(8,128)S(1)} %bitcast.145), channel_id=1, source_target_pairs={{4,0},{8,4},{12,8},{16,12},{20,16},{24,20},{28,24},{32,28},{36,32}... | collective-permute-start | bytes 3080 | tf_op jit(solution)/shard_map/ppermute | solution.py:16
  201.2 1.7 fusion.10
  202.9 1.9 collective-permute-start.11
  204.9 1.7 fusion.6
  207.4 10.1 %collective-permute-done.11 = f32[16,16]{1,0:T(8,128)S(1)} collective-permute-done((f32[16,16]{1,0:T(8,128)S(1)}, f32[16,16]{1,0:T(8,128)S(1)}, u32[]{:S(2)}, u32[]{:S(2)}) %collective-permute-start.11) | collective-permute-done | bytes 1056 | tf_op jit(solution)/shard_map/ppermute | solution.py:16
  217.8 8.1 %all_to_all.38 = f32[4,1,576]{2,1,0:T(1,128)S(1)} all-to-all(f32[4,1,576]{2,1,0:T(1,128)S(1)} %reshape.130), channel_id=1, replica_groups=mesh['sta'=128,'cell'=4] {'cell'}, dimensions={0} | all-to-all | bytes 18432 | tf_op jit(solution)/shard_map/all_to_all | solution.py:26
  226.5 0.7 reduce
  (57 shorter events, 8.8 us)
Async XLA Ops:
  0.0 68.3 %copy-start = (bf16[128,128]{1,0:T(8,128)(2,1)S(1)}, bf16[128,128]{1,0:T(8,128)(2,1)}, u32[]{:S(2)}) copy-start(bf16[128,128]{1,0:T(8,128)(2,1)} %param.15) | copy-start | bytes 98308
  0.0 61.5 %all-to-all-start = ((bf16[16,52,512]{2,0,1:T(8,128)(2,1)}), bf16[16,52,512]{2,0,1:T(8,128)(2,1)S(1)}, u32[]{:S(2)}, u32[]{:S(2)}) async-start(bf16[16,52,512]{2,0,1:T(8,128)(2,1)} %param.10), calls=%async_computation | async-start | bytes 1703936 | tf_op jit(solution)/shard_map/all_to_all | solution.py:82
  7.4 41.8 %collective-permute-start.4 = (bf16[16,52,512]{2,0,1:T(8,128)(2,1)}, bf16[16,52,512]{2,0,1:T(8,128)(2,1)S(1)}, u32[]{:S(2)}, u32[]{:S(2)}) collective-permute-start(bf16[16,52,512]{2,0,1:T(8,128)(2,1)} %param.10), channel_id=1, source_target_pairs={{508,0},{0,4},{4,8},{8,12},{12,16},{16,20},{20,24},{24,28},{28,32}... | collective-permute-start | bytes 2555912 | tf_op jit(solution)/shard_map/ppermute | solution.py:16
  9.3 14.2 %collective-permute-start = (s32[1,52]{1,0:T(1,128)}, s32[1,52]{1,0:T(1,128)S(1)}, u32[]{:S(2)}, u32[]{:S(2)}) collective-permute-start(s32[1,52]{1,0:T(1,128)} %param.11), channel_id=1, source_target_pairs={{508,0},{0,4},{4,8},{8,12},{12,16},{16,20},{20,24},{24,28},{28,32}... | collective-permute-start | bytes 632 | tf_op jit(solution)/shard_map/ppermute | solution.py:16
  23.5 10.0 %collective-permute-start.1 = (s32[1,52]{1,0:T(1,128)S(1)}, s32[1,52]{1,0:T(1,128)S(1)}, u32[]{:S(2)}, u32[]{:S(2)}) collective-permute-start(s32[1,52]{1,0:T(1,128)S(1)} %collective-permute-done), channel_id=1, source_target_pairs={{508,0},{0,4},{4,8},{8,12},{12,16},{16,20},{20,24},{24,28},{28,32}... | collective-permute-start | bytes 632 | tf_op jit(solution)/shard_map/ppermute | solution.py:16
  33.5 66.4 %collective-permute-start.2 = (s32[1,52]{1,0:T(1,128)S(1)}, s32[1,52]{1,0:T(1,128)S(1)}, u32[]{:S(2)}, u32[]{:S(2)}) collective-permute-start(s32[1,52]{1,0:T(1,128)S(1)} %collective-permute-done.1), channel_id=1, source_target_pairs={{508,0},{0,4},{4,8},{8,12},{12,16},{16,20},{20,24},{24,28},{28,32}... | collective-permute-start | bytes 632 | tf_op jit(solution)/shard_map/ppermute | solution.py:16
  49.2 24.0 %copy-start.3 = (bf16[16,52,512]{2,0,1:T(8,128)(2,1)}, bf16[16,52,512]{2,0,1:T(8,128)(2,1)S(1)}, u32[]{:S(2)}) copy-start(bf16[16,52,512]{2,0,1:T(8,128)(2,1)S(1)} %collective-permute-done.4) | copy-start | bytes 2555908
  49.2 52.6 %collective-permute-start.5 = (bf16[16,52,512]{2,0,1:T(8,128)(2,1)S(1)}, bf16[16,52,512]{2,0,1:T(8,128)(2,1)}, u32[]{:S(2)}, u32[]{:S(2)}) collective-permute-start(bf16[16,52,512]{2,0,1:T(8,128)(2,1)S(1)} %collective-permute-done.4), channel_id=1, source_target_pairs={{508,0},{0,4},{4,8},{8,12},{12,16},{16,20},{20,24},{24,28},{28,32}... | collective-permute-start | bytes 2555912 | tf_op jit(solution)/shard_map/ppermute | solution.py:16
  94.0 27.5 %all-to-all-start.1 = ((bf16[4,2,53248]{2,1,0:T(2,128)(2,1)}), bf16[4,2,53248]{2,1,0:T(2,128)(2,1)S(1)}, u32[]{:S(2)}, u32[]{:S(2)}) async-start(bf16[4,2,53248]{2,1,0:T(2,128)(2,1)} %reshape.128), calls=%async_computation.1 | async-start | bytes 1703936 | tf_op jit(solution)/shard_map/all_to_all | solution.py:80
  99.9 4.9 %collective-permute-start.3 = (s32[1,52]{1,0:T(1,128)S(1)}, s32[1,52]{1,0:T(1,128)S(1)}, u32[]{:S(2)}, u32[]{:S(2)}) collective-permute-start(s32[1,52]{1,0:T(1,128)S(1)} %collective-permute-done.2), channel_id=1, source_target_pairs={{508,0},{0,4},{4,8},{8,12},{12,16},{16,20},{20,24},{24,28},{28,32}... | collective-permute-start | bytes 632 | tf_op jit(solution)/shard_map/ppermute | solution.py:16
  101.8 39.2 %collective-permute-start.6 = (bf16[16,52,512]{2,0,1:T(8,128)(2,1)}, bf16[16,52,512]{2,0,1:T(8,128)(2,1)}, u32[]{:S(2)}, u32[]{:S(2)}) collective-permute-start(bf16[16,52,512]{2,0,1:T(8,128)(2,1)} %collective-permute-done.5), channel_id=1, source_target_pairs={{508,0},{0,4},{4,8},{8,12},{12,16},{16,20},{20,24},{24,28},{28,32}... | collective-permute-start | bytes 2555912 | tf_op jit(solution)/shard_map/ppermute | solution.py:16
  129.3 9.5 %copy-start.2 = (s32[1,52]{1,0:T(1,128)S(1)}, s32[1,52]{1,0:T(1,128)}, u32[]{:S(2)}) copy-start(s32[1,52]{1,0:T(1,128)} %param.11) | copy-start | bytes 628
  129.3 13.7 %copy-start.1 = (bf16[16,16]{1,0:T(8,128)(2,1)S(1)}, bf16[16,16]{1,0:T(8,128)(2,1)}, u32[]{:S(2)}) copy-start(bf16[16,16]{1,0:T(8,128)(2,1)} %param.13) | copy-start | bytes 1540
  141.0 60.1 %collective-permute-start.7 = (bf16[16,52,512]{2,0,1:T(8,128)(2,1)}, bf16[16,52,512]{2,0,1:T(8,128)(2,1)}, u32[]{:S(2)}, u32[]{:S(2)}) collective-permute-start(bf16[16,52,512]{2,0,1:T(8,128)(2,1)} %collective-permute-done.6), channel_id=1, source_target_pairs={{508,0},{0,4},{4,8},{8,12},{12,16},{16,20},{20,24},{24,28},{28,32}... | collective-permute-start | bytes 2555912 | tf_op jit(solution)/shard_map/ppermute | solution.py:16
  188.3 18.5 %collective-permute-start.10 = (f32[16,16]{1,0:T(8,128)S(1)}, f32[16,16]{1,0:T(8,128)S(1)}, u32[]{:S(2)}, u32[]{:S(2)}) collective-permute-start(f32[16,16]{1,0:T(8,128)S(1)} %bitcast.143), channel_id=1, source_target_pairs={{12,0},{16,4},{20,8},{24,12},{28,16},{32,20},{36,24},{40,28},{44,3... | collective-permute-start | bytes 3080 | tf_op jit(solution)/shard_map/ppermute | solution.py:16
  192.6 14.9 %collective-permute-start.9 = (f32[16,16]{1,0:T(8,128)S(1)}, f32[16,16]{1,0:T(8,128)S(1)}, u32[]{:S(2)}, u32[]{:S(2)}) collective-permute-start(f32[16,16]{1,0:T(8,128)S(1)} %bitcast.144), channel_id=1, source_target_pairs={{8,0},{12,4},{16,8},{20,12},{24,16},{28,20},{32,24},{36,28},{40,32... | collective-permute-start | bytes 3080 | tf_op jit(solution)/shard_map/ppermute | solution.py:16
  196.8 10.6 %collective-permute-start.8 = (f32[16,16]{1,0:T(8,128)S(1)}, f32[16,16]{1,0:T(8,128)S(1)}, u32[]{:S(2)}, u32[]{:S(2)}) collective-permute-start(f32[16,16]{1,0:T(8,128)S(1)} %bitcast.145), channel_id=1, source_target_pairs={{4,0},{8,4},{12,8},{16,12},{20,16},{24,20},{28,24},{32,28},{36,32}... | collective-permute-start | bytes 3080 | tf_op jit(solution)/shard_map/ppermute | solution.py:16
  202.9 14.6 %collective-permute-start.11 = (f32[16,16]{1,0:T(8,128)S(1)}, f32[16,16]{1,0:T(8,128)S(1)}, u32[]{:S(2)}, u32[]{:S(2)}) collective-permute-start(f32[16,16]{1,0:T(8,128)S(1)} %bitcast.146), channel_id=1, source_target_pairs={{16,0},{20,4},{24,8},{28,12},{32,16},{36,20},{40,24},{44,28},{48,3... | collective-permute-start | bytes 3080 | tf_op jit(solution)/shard_map/ppermute | solution.py:16
where the time goes:
time: 229 us; the launch traced here: 228 us
  local copies, waits for them, and re-layouts  90 us (39%)
  starting transfers between devices  75.1 us (33%)
  waiting for transfers between devices  29 us (13%)
  matrix products  19.2 us (8%)
  blocking collectives  8.13 us (4%)
  between operations  3.47 us (2%)
  other arithmetic  2.69 us (1%)
    ppermute x12, starting transfers between devices, from_behind(): return lax.ppermute(block, axis, route)  61.9 us
    all_to_all x1, waiting for transfers between devices, body(): lax.all_to_all(smooth_depth(lax.all_to_all(sensitivity, 'cell', split_axi...  16.7 us
    unnamed x12, local copies, waits for them, and re-layouts  16.3 us
    broadcast_in_dim x4, local copies, waits for them, and re-layouts, smooth_plane(): lax.map(smooth_group, grouped).reshape(row_count, tile_count, slab_width)  14.3 us
    reshape x1, local copies, waits for them, and re-layouts, smooth_depth(): smoothed.astype(jnp.bfloat16).reshape(row_count, tile_count, slab_width)  12.5 us
    ppermute x12, waiting for transfers between devices, from_behind(): return lax.ppermute(block, axis, route)  12.3 us
    reshape x8, local copies, waits for them, and re-layouts, smooth_group(): row_group.reshape(group_rows, cells_across, blocks_along, slab_width // T...  11.4 us
    all_to_all x2, local copies, waits for them, and re-layouts, body(): lax.all_to_all(smooth_depth(lax.all_to_all(sensitivity, 'cell', split_axi...  9.47 us
  transfers between devices with their start and end apart: 14, of which 5 were waited for; matrix products, arithmetic and copies ran while one was open for 48% of the time, Pallas kernels for 0%

commit v1 on v0

--- a/solution.py
+++ b/solution.py
@@ -77,14 +77,25 @@
 
 def body(sensitivity, footprint, linked, smooth_x, smooth_y, smooth_z):
     own_tiles = footprint[0]
-    depth_rows = lax.all_to_all(
-        smooth_depth(
-            lax.all_to_all(sensitivity, "cell", split_axis=1, concat_axis=2, tiled=True), smooth_z
+    depth_rows = jnp.concatenate(
+        lax.all_to_all(
+            jnp.stack(
+                jnp.split(
+                    smooth_depth(
+                        lax.all_to_all(
+                            sensitivity, "cell", split_axis=1, concat_axis=2, tiled=True
+                        ),
+                        smooth_z,
+                    ),
+                    lax.axis_size("cell"),
+                    axis=2,
+                )
+            ),
+            "cell",
+            0,
+            0,
         ),
-        "cell",
-        split_axis=2,
-        concat_axis=1,
-        tiled=True,
+        axis=1,
     )
     grid_rows = spread_tiles(depth_rows, own_tiles)
     smoothed = smooth_plane(grid_rows, smooth_x, smooth_y)

time: 229 us -> 221 us (0.965)
  local copies, waits for them, and re-layouts: 90 us -> 69.3 us
  waiting for transfers between devices: 29 us -> 38.2 us
  blocking collectives: 8.13 us -> 11.7 us
    unnamed x12, local copies, waits for them, and re-layouts: 16.3 us -> 0.21 us
    all_to_all x2 -> x0, local copies, waits for them, and re-layouts: 9.47 us -> none  [body(): lax.all_to_all(smooth_depth(lax.all_to_all(sensitivity, 'cell', split_axi...]
    ppermute x12, waiting for transfers between devices: 12.3 us -> 21.5 us  [from_behind(): return lax.ppermute(block, axis, route)]
    convert_element_type x0 -> x1, local copies, waits for them, and re-layouts: none -> 5.08 us  [smooth_depth(): smoothed.astype(jnp.bfloat16).reshape(row_count, tile_count, slab_width)]
    all_to_all x1, blocking collectives: 8.13 us -> 11.7 us  [sent_and_summed(): lax.all_to_all(blocks, axis, split_axis=0, concat_axis=0, tiled=True)]
  transfers between devices with their start and end apart: 14 -> 14, of which waited for: 5 -> 6; matrix products, arithmetic and copies ran while one was open for 48% -> 40% of each run, Pallas kernels for 0% -> 0%
where the time goes in v1:
time: 221 us; the launch traced here: 220 us
  starting transfers between devices  75.5 us (34%)
  local copies, waits for them, and re-layouts  69.3 us (31%)
  waiting for transfers between devices  38.2 us (17%)
  matrix products  18.1 us (8%)
  blocking collectives  11.7 us (5%)
  other arithmetic  3.71 us (2%)
  between operations  3.26 us (1%)
    ppermute x12, starting transfers between devices, from_behind(): return lax.ppermute(block, axis, route)  62.1 us
    ppermute x12, waiting for transfers between devices, from_behind(): return lax.ppermute(block, axis, route)  21.5 us
    all_to_all x1, waiting for transfers between devices, body(): lax.all_to_all(jnp.stack(jnp.split(smooth_depth(lax.all_to_all(sensitivit...  16.7 us
    broadcast_in_dim x4, local copies, waits for them, and re-layouts, smooth_plane(): lax.map(smooth_group, grouped).reshape(row_count, tile_count, slab_width)  14.3 us
    reshape x1, local copies, waits for them, and re-layouts, smooth_depth(): smoothed.astype(jnp.bfloat16).reshape(row_count, tile_count, slab_width)  12.3 us
    all_to_all x1, blocking collectives, sent_and_summed(): lax.all_to_all(blocks, axis, split_axis=0, concat_axis=0, tiled=True)  11.7 us
    reshape x8, local copies, waits for them, and re-layouts, smooth_group(): row_group.reshape(group_rows, cells_across, blocks_along, slab_width // T...  11.4 us
    dot_general x5, matrix products, pair_tile(): lax.dot_general(picked, partner, (((1,), (1,)), ((), ())), preferred_elem...  7.46 us
  transfers between devices with their start and end apart: 14, of which 6 were waited for; matrix products, arithmetic and copies ran while one was open for 40% of the time, Pallas kernels for 0%

profile of v1, /device:TPU:62, one launch (start us, length us, event | category | flops | bytes accessed | tf_op | source)
XLA Modules:
  0.0 220.1 jit_solution(9820732436093392911)
XLA Ops:
  0.0 7.4 %all-to-all-start = ((bf16[16,52,512]{2,0,1:T(8,128)(2,1)}), bf16[16,52,512]{2,0,1:T(8,128)(2,1)S(1)}, u32[]{:S(2)}, u32[]{:S(2)}) async-start(bf16[16,52,512]{2,0,1:T(8,128)(2,1)} %param.10), calls=%async_computation | async-start | bytes 1703936 | tf_op jit(solution)/shard_map/all_to_all | solution.py:85
  7.4 1.9 collective-permute-start.4
  9.3 7.4 %collective-permute-start = (s32[1,52]{1,0:T(1,128)}, s32[1,52]{1,0:T(1,128)S(1)}, u32[]{:S(2)}, u32[]{:S(2)}) collective-permute-start(s32[1,52]{1,0:T(1,128)} %param.11), channel_id=1, source_target_pairs={{508,0},{0,4},{4,8},{8,12},{12,16},{16,20},{20,24},{24,28},{28,32}... | collective-permute-start | bytes 632 | tf_op jit(solution)/shard_map/ppermute | solution.py:16
  16.8 0.8 reshape.67
  17.6 1.4 fusion.41
  20.8 0.7 compare_select_fusion
  21.5 0.7 compare_and_fusion
  23.3 9.4 %collective-permute-start.1 = (s32[1,52]{1,0:T(1,128)S(1)}, s32[1,52]{1,0:T(1,128)S(1)}, u32[]{:S(2)}, u32[]{:S(2)}) collective-permute-start(s32[1,52]{1,0:T(1,128)S(1)} %collective-permute-done), channel_id=1, source_target_pairs={{508,0},{0,4},{4,8},{8,12},{12,16},{16,20},{20,24},{24,28},{28,32}... | collective-permute-start | bytes 632 | tf_op jit(solution)/shard_map/ppermute | solution.py:16
  32.7 0.8 collective-permute-done.1
  33.5 15.7 %collective-permute-start.2 = (s32[1,52]{1,0:T(1,128)S(1)}, s32[1,52]{1,0:T(1,128)S(1)}, u32[]{:S(2)}, u32[]{:S(2)}) collective-permute-start(s32[1,52]{1,0:T(1,128)S(1)} %collective-permute-done.1), channel_id=1, source_target_pairs={{508,0},{0,4},{4,8},{8,12},{12,16},{16,20},{20,24},{24,28},{28,32}... | collective-permute-start | bytes 632 | tf_op jit(solution)/shard_map/ppermute | solution.py:16
  49.2 12.3 %collective-permute-start.5 = (bf16[16,52,512]{2,0,1:T(8,128)(2,1)S(1)}, bf16[16,52,512]{2,0,1:T(8,128)(2,1)}, u32[]{:S(2)}, u32[]{:S(2)}) collective-permute-start(bf16[16,52,512]{2,0,1:T(8,128)(2,1)S(1)} %collective-permute-done.4), channel_id=1, source_target_pairs={{508,0},{0,4},{4,8},{8,12},{12,16},{16,20},{20,24},{24,28},{28,32}... | collective-permute-start | bytes 2555912 | tf_op jit(solution)/shard_map/ppermute | solution.py:16
  61.5 0.7 copy.69
  62.2 6.1 %reshape.62 = bf16[16,13,128,16]{3,2,1,0:T(8,128)(2,1)} reshape(bf16[16,13,4,512]{3,2,1,0:T(4,128)(2,1)S(1)} %bitcast.146) | data formatting | bytes 1703936 | tf_op jit(solution)/shard_map/reshape | solution.py:41
  68.3 4.8 %fusion.5 = bf16[16,13,128,16]{2,3,1,0:T(8,128)(2,1)S(1)} fusion(bf16[16,13,128,16]{3,2,1,0:T(8,128)(2,1)} %reshape.62, bf16[128,128]{1,0:T(8,128)(2,1)S(1)} %copy-done), kind=kOutput, calls=%fused_computation.16 | convolution fusion | flops 109477888 | bytes 1736704 | tf_op jit(solution)/shard_map/rtzc,wz->rtwc/dot_general | solution.py:42
  73.1 5.1 %copy.36 = bf16[16,13,128,16]{3,2,0,1:T(8,128)(2,1)} copy(bf16[16,13,128,16]{2,3,1,0:T(8,128)(2,1)S(1)} %fusion.5) | data formatting | bytes 1703936 | tf_op jit(solution)/shard_map/convert_element_type | solution.py:43
  78.2 12.3 %reshape.63 = bf16[16,13,2048]{2,0,1:T(8,128)(2,1)S(1)} reshape(bf16[16,13,128,16]{3,2,0,1:T(8,128)(2,1)} %copy.36) | data formatting | bytes 1703936 | tf_op jit(solution)/shard_map/reshape | solution.py:43
  90.7 1.0 pad_maximum_fusion
  91.7 6.0 %all-to-all-start.1 = ((bf16[4,16,13,512]{3,1,2,0:T(8,128)(2,1)}), bf16[4,16,13,512]{3,1,2,0:T(8,128)(2,1)S(1)}, u32[]{:S(2)}, u32[]{:S(2)}) async-start(bf16[4,16,13,512]{3,1,2,0:T(8,128)(2,1)} %pad_maximum_fusion), calls=%async_computation.1 | async-start | bytes 1703936 | tf_op jit(solution)/shard_map/all_to_all | solution.py:81
  97.7 1.9 collective-permute-start.3
  99.7 1.9 collective-permute-start.6
  101.6 1.0 collective-permute-done.3
  102.6 16.7 %all-to-all-done.1 = bf16[4,16,13,512]{3,1,2,0:T(8,128)(2,1)S(1)} async-done(((bf16[4,16,13,512]{3,1,2,0:T(8,128)(2,1)}), bf16[4,16,13,512]{3,1,2,0:T(8,128)(2,1)S(1)}, u32[]{:S(2)}, u32[]{:S(2)}) %all-to-all-start.1) | async-done | bytes 852000 | tf_op jit(solution)/shard_map/all_to_all | solution.py:81
  119.4 2.3 %convolution_convert_fusion.1 = bf16[64,16,512]{2,0,1:T(8,128)(2,1)} fusion(bf16[16,52,512]{2,0,1:T(8,128)(2,1)S(1)} %bitcast.144, s32[52]{0:T(128)S(1)} %bitcast.153), kind=kOutput, calls=%fused_computation.14 | convolution fusion | flops 55053568 | bytes 1900752 | tf_op jit(solution)/shard_map/rfk,ft->rtk/dot_general | solution.py:34
  121.7 2.1 collective-permute-start.7
  123.8 40.5 %while.10 = (s32[]{:T(128)}, bf16[4,4,64,512]{3,2,1,0:T(8,128)(2,1)}, bf16[4,4,64,512]{3,2,1,0:T(8,128)(2,1)}, bf16[16,16]{1,0:T(8,128)(2,1)S(1)}, bf16[4,16,4,16]{3,1,2,0:T(8,128)(2,1)S(1)}, /*index=5*/s32[]{:T(128)}) while((s32[]{:T(128)}, bf16[4,4,64,512]{3,2,1,0:T(8,128)(2,1)}, bf16[4,4,64,512]{3,2,1,0:T(8,128)(2,1)}, ...), condition=%wide.region_1.2_spmd, body=%wide.region_0.1_spmd.sunk | while | flops 21233664 | bytes 4203593 | solution.py:66
  123.8 1.0 constant_dynamic-slice_fusion.2
  124.8 1.7 reshape.139
  126.5 1.2 copy.75
  128.5 1.0 copy.76
  129.6 3.6 %broadcast_in_dim.31 = bf16[1,4,64,512]{3,2,1,0:T(8,128)(2,1)S(1)} reshape(bf16[4,16,4,32,16]{4,3,2,1,0:T(8,128)(2,1)S(1)} %copy.76) | data formatting | bytes 524288 | tf_op jit(solution)/shard_map/while/body/jit(dynamic_update_index_in_dim)/broadcast_in_dim | solution.py:66
  133.2 0.7 constant_dynamic-update-slice_fusion.2
  133.9 1.0 constant_dynamic-slice_fusion.2
  134.9 1.7 reshape.139
  136.6 1.2 copy.75
  138.7 1.0 copy.76
  139.7 3.6 %broadcast_in_dim.31 = bf16[1,4,64,512]{3,2,1,0:T(8,128)(2,1)S(1)} reshape(bf16[4,16,4,32,16]{4,3,2,1,0:T(8,128)(2,1)S(1)} %copy.76) | data formatting | bytes 524288 | tf_op jit(solution)/shard_map/while/body/jit(dynamic_update_index_in_dim)/broadcast_in_dim | solution.py:66
  143.3 0.7 constant_dynamic-update-slice_fusion.2
  144.0 1.0 constant_dynamic-slice_fusion.2
  145.0 1.7 reshape.139
  146.7 1.2 copy.75
  148.8 1.0 copy.76
  149.8 3.6 %broadcast_in_dim.31 = bf16[1,4,64,512]{3,2,1,0:T(8,128)(2,1)S(1)} reshape(bf16[4,16,4,32,16]{4,3,2,1,0:T(8,128)(2,1)S(1)} %copy.76) | data formatting | bytes 524288 | tf_op jit(solution)/shard_map/while/body/jit(dynamic_update_index_in_dim)/broadcast_in_dim | solution.py:66
  153.4 0.7 constant_dynamic-update-slice_fusion.2
  154.1 1.0 constant_dynamic-slice_fusion.2
  155.1 1.7 reshape.139
  156.8 1.2 copy.75
  158.9 1.0 copy.76
  159.9 3.6 %broadcast_in_dim.31 = bf16[1,4,64,512]{3,2,1,0:T(8,128)(2,1)S(1)} reshape(bf16[4,16,4,32,16]{4,3,2,1,0:T(8,128)(2,1)S(1)} %copy.76) | data formatting | bytes 524288 | tf_op jit(solution)/shard_map/while/body/jit(dynamic_update_index_in_dim)/broadcast_in_dim | solution.py:66
  163.5 0.7 constant_dynamic-update-slice_fusion.2
  164.2 1.8 copy.59
  166.0 0.6 gather_fusion
  167.3 1.7 fusion.9
  169.0 1.9 collective-permute-start.10
  171.6 1.7 fusion.8
  173.3 1.9 collective-permute-start.9
  175.9 1.7 fusion.7
  177.6 3.7 %collective-permute-start.8 = (f32[16,16]{1,0:T(8,128)S(1)}, f32[16,16]{1,0:T(8,128)S(1)}, u32[]{:S(2)}, u32[]{:S(2)}) collective-permute-start(f32[16,16]{1,0:T(8,128)S(1)} %bitcast.151), channel_id=1, source_target_pairs={{4,0},{8,4},{12,8},{16,12},{20,16},{24,20},{28,24},{32,28},{36,32}... | collective-permute-start | bytes 3080 | tf_op jit(solution)/shard_map/ppermute | solution.py:16
  181.9 1.8 fusion.10
  183.8 1.9 collective-permute-start.11
  186.5 1.7 collective-permute-done.9
  188.2 1.6 collective-permute-done.8
  189.8 16.4 %collective-permute-done.11 = f32[16,16]{1,0:T(8,128)S(1)} collective-permute-done((f32[16,16]{1,0:T(8,128)S(1)}, f32[16,16]{1,0:T(8,128)S(1)}, u32[]{:S(2)}, u32[]{:S(2)}) %collective-permute-start.11) | collective-permute-done | bytes 1056 | tf_op jit(solution)/shard_map/ppermute | solution.py:16
  206.5 11.7 %all_to_all.25 = f32[4,1,576]{2,1,0:T(1,128)S(1)} all-to-all(f32[4,1,576]{2,1,0:T(1,128)S(1)} %reshape.136), channel_id=1, replica_groups=mesh['sta'=128,'cell'=4] {'cell'}, dimensions={0} | all-to-all | bytes 18432 | tf_op jit(solution)/shard_map/all_to_all | solution.py:26
  218.7 0.7 reduce
  (58 shorter events, 8.6 us)
Async XLA Ops:
  0.0 68.3 %copy-start = (bf16[128,128]{1,0:T(8,128)(2,1)S(1)}, bf16[128,128]{1,0:T(8,128)(2,1)}, u32[]{:S(2)}) copy-start(bf16[128,128]{1,0:T(8,128)(2,1)} %param.15) | copy-start | bytes 98308
  0.0 61.5 %all-to-all-start = ((bf16[16,52,512]{2,0,1:T(8,128)(2,1)}), bf16[16,52,512]{2,0,1:T(8,128)(2,1)S(1)}, u32[]{:S(2)}, u32[]{:S(2)}) async-start(bf16[16,52,512]{2,0,1:T(8,128)(2,1)} %param.10), calls=%async_computation | async-start | bytes 1703936 | tf_op jit(solution)/shard_map/all_to_all | solution.py:85
  7.4 41.8 %collective-permute-start.4 = (bf16[16,52,512]{2,0,1:T(8,128)(2,1)}, bf16[16,52,512]{2,0,1:T(8,128)(2,1)S(1)}, u32[]{:S(2)}, u32[]{:S(2)}) collective-permute-start(bf16[16,52,512]{2,0,1:T(8,128)(2,1)} %param.10), channel_id=1, source_target_pairs={{508,0},{0,4},{4,8},{8,12},{12,16},{16,20},{20,24},{24,28},{28,32}... | collective-permute-start | bytes 2555912 | tf_op jit(solution)/shard_map/ppermute | solution.py:16
  9.3 13.9 %collective-permute-start = (s32[1,52]{1,0:T(1,128)}, s32[1,52]{1,0:T(1,128)S(1)}, u32[]{:S(2)}, u32[]{:S(2)}) collective-permute-start(s32[1,52]{1,0:T(1,128)} %param.11), channel_id=1, source_target_pairs={{508,0},{0,4},{4,8},{8,12},{12,16},{16,20},{20,24},{24,28},{28,32}... | collective-permute-start | bytes 632 | tf_op jit(solution)/shard_map/ppermute | solution.py:16
  23.3 10.2 %collective-permute-start.1 = (s32[1,52]{1,0:T(1,128)S(1)}, s32[1,52]{1,0:T(1,128)S(1)}, u32[]{:S(2)}, u32[]{:S(2)}) collective-permute-start(s32[1,52]{1,0:T(1,128)S(1)} %collective-permute-done), channel_id=1, source_target_pairs={{508,0},{0,4},{4,8},{8,12},{12,16},{16,20},{20,24},{24,28},{28,32}... | collective-permute-start | bytes 632 | tf_op jit(solution)/shard_map/ppermute | solution.py:16
  33.5 64.2 %collective-permute-start.2 = (s32[1,52]{1,0:T(1,128)S(1)}, s32[1,52]{1,0:T(1,128)S(1)}, u32[]{:S(2)}, u32[]{:S(2)}) collective-permute-start(s32[1,52]{1,0:T(1,128)S(1)} %collective-permute-done.1), channel_id=1, source_target_pairs={{508,0},{0,4},{4,8},{8,12},{12,16},{16,20},{20,24},{24,28},{28,32}... | collective-permute-start | bytes 632 | tf_op jit(solution)/shard_map/ppermute | solution.py:16
  49.2 19.1 %copy-start.4 = (bf16[16,52,512]{2,0,1:T(8,128)(2,1)}, bf16[16,52,512]{2,0,1:T(8,128)(2,1)S(1)}, u32[]{:S(2)}) copy-start(bf16[16,52,512]{2,0,1:T(8,128)(2,1)S(1)} %collective-permute-done.4) | copy-start | bytes 2555908
  49.2 50.5 %collective-permute-start.5 = (bf16[16,52,512]{2,0,1:T(8,128)(2,1)S(1)}, bf16[16,52,512]{2,0,1:T(8,128)(2,1)}, u32[]{:S(2)}, u32[]{:S(2)}) collective-permute-start(bf16[16,52,512]{2,0,1:T(8,128)(2,1)S(1)} %collective-permute-done.4), channel_id=1, source_target_pairs={{508,0},{0,4},{4,8},{8,12},{12,16},{16,20},{20,24},{24,28},{28,32}... | collective-permute-start | bytes 2555912 | tf_op jit(solution)/shard_map/ppermute | solution.py:16
  90.7 28.7 %copy-start.3 = (s32[1,52]{1,0:T(1,128)S(1)}, s32[1,52]{1,0:T(1,128)}, u32[]{:S(2)}) copy-start(s32[1,52]{1,0:T(1,128)} %param.11) | copy-start | bytes 628
  91.7 32.1 %copy-start.2 = (bf16[16,16]{1,0:T(8,128)(2,1)S(1)}, bf16[16,16]{1,0:T(8,128)(2,1)}, u32[]{:S(2)}) copy-start(bf16[16,16]{1,0:T(8,128)(2,1)} %param.13) | copy-start | bytes 1540
  91.7 27.7 %all-to-all-start.1 = ((bf16[4,16,13,512]{3,1,2,0:T(8,128)(2,1)}), bf16[4,16,13,512]{3,1,2,0:T(8,128)(2,1)S(1)}, u32[]{:S(2)}, u32[]{:S(2)}) async-start(bf16[4,16,13,512]{3,1,2,0:T(8,128)(2,1)} %pad_maximum_fusion), calls=%async_computation.1 | async-start | bytes 1703936 | tf_op jit(solution)/shard_map/all_to_all | solution.py:81
  97.7 4.9 %collective-permute-start.3 = (s32[1,52]{1,0:T(1,128)S(1)}, s32[1,52]{1,0:T(1,128)S(1)}, u32[]{:S(2)}, u32[]{:S(2)}) collective-permute-start(s32[1,52]{1,0:T(1,128)S(1)} %collective-permute-done.2), channel_id=1, source_target_pairs={{508,0},{0,4},{4,8},{8,12},{12,16},{16,20},{20,24},{24,28},{28,32}... | collective-permute-start | bytes 632 | tf_op jit(solution)/shard_map/ppermute | solution.py:16
  99.7 22.0 %collective-permute-start.6 = (bf16[16,52,512]{2,0,1:T(8,128)(2,1)}, bf16[16,52,512]{2,0,1:T(8,128)(2,1)}, u32[]{:S(2)}, u32[]{:S(2)}) collective-permute-start(bf16[16,52,512]{2,0,1:T(8,128)(2,1)} %collective-permute-done.5), channel_id=1, source_target_pairs={{508,0},{0,4},{4,8},{8,12},{12,16},{16,20},{20,24},{24,28},{28,32}... | collective-permute-start | bytes 2555912 | tf_op jit(solution)/shard_map/ppermute | solution.py:16
  121.7 60.2 %collective-permute-start.7 = (bf16[16,52,512]{2,0,1:T(8,128)(2,1)}, bf16[16,52,512]{2,0,1:T(8,128)(2,1)}, u32[]{:S(2)}, u32[]{:S(2)}) collective-permute-start(bf16[16,52,512]{2,0,1:T(8,128)(2,1)} %collective-permute-done.6), channel_id=1, source_target_pairs={{508,0},{0,4},{4,8},{8,12},{12,16},{16,20},{20,24},{24,28},{28,32}... | collective-permute-start | bytes 2555912 | tf_op jit(solution)/shard_map/ppermute | solution.py:16
  169.0 17.5 %collective-permute-start.10 = (f32[16,16]{1,0:T(8,128)S(1)}, f32[16,16]{1,0:T(8,128)S(1)}, u32[]{:S(2)}, u32[]{:S(2)}) collective-permute-start(f32[16,16]{1,0:T(8,128)S(1)} %bitcast.149), channel_id=1, source_target_pairs={{12,0},{16,4},{20,8},{24,12},{28,16},{32,20},{36,24},{40,28},{44,3... | collective-permute-start | bytes 3080 | tf_op jit(solution)/shard_map/ppermute | solution.py:16
  173.3 14.9 %collective-permute-start.9 = (f32[16,16]{1,0:T(8,128)S(1)}, f32[16,16]{1,0:T(8,128)S(1)}, u32[]{:S(2)}, u32[]{:S(2)}) collective-permute-start(f32[16,16]{1,0:T(8,128)S(1)} %bitcast.150), channel_id=1, source_target_pairs={{8,0},{12,4},{16,8},{20,12},{24,16},{28,20},{32,24},{36,28},{40,32... | collective-permute-start | bytes 3080 | tf_op jit(solution)/shard_map/ppermute | solution.py:16
  177.6 12.2 %collective-permute-start.8 = (f32[16,16]{1,0:T(8,128)S(1)}, f32[16,16]{1,0:T(8,128)S(1)}, u32[]{:S(2)}, u32[]{:S(2)}) collective-permute-start(f32[16,16]{1,0:T(8,128)S(1)} %bitcast.151), channel_id=1, source_target_pairs={{4,0},{8,4},{12,8},{16,12},{20,16},{24,20},{28,24},{32,28},{36,32}... | collective-permute-start | bytes 3080 | tf_op jit(solution)/shard_map/ppermute | solution.py:16
  181.9 3.8 %copy-start.1 = (bf16[16,52,512]{2,0,1:T(8,128)(2,1)S(1)}, bf16[16,52,512]{2,0,1:T(8,128)(2,1)}, u32[]{:S(2)}) copy-start(bf16[16,52,512]{2,0,1:T(8,128)(2,1)} %param.10) | copy-start | bytes 2555908
  183.8 22.4 %collective-permute-start.11 = (f32[16,16]{1,0:T(8,128)S(1)}, f32[16,16]{1,0:T(8,128)S(1)}, u32[]{:S(2)}, u32[]{:S(2)}) collective-permute-start(f32[16,16]{1,0:T(8,128)S(1)} %bitcast.152), channel_id=1, source_target_pairs={{16,0},{20,4},{24,8},{28,12},{32,16},{36,20},{40,24},{44,28},{48,3... | collective-permute-start | bytes 3080 | tf_op jit(solution)/shard_map/ppermute | solution.py:16
